TPU v7x, 256 devices: a whole 4x4x8 slice. The times are simulated.
256 devices in a mesh: seq: 16 (over z, core), exp: 16 (over y, x).
Axes of the slice: x: 4, y: 4, z: 8, core: 2. Of those that a mesh axis runs over, the one named last changes fastest.
Arguments:
- tokens: bfloat16 [16, 2048, 2048], P('exp', 'seq'), may hold values from -10 to 10
- head_inputs: bfloat16 [16, 2048, 6144], P('exp', 'seq'), may hold values from -100 to 100
- window_ids: int32 [16, 2048], P('exp', 'seq'), may hold values from 0 to 3, never falling along the last dimension, each value on 1 to 1024 neighbouring positions
- modulation: float32 [16, 4, 2048], P('exp'), may hold values from -3 to 3
- out_weight: bfloat16 [2048, 2048], replicated, may hold values from -0.125 to 0.125
- expert_in: bfloat16 [16, 2048, 4096], P('exp', None, 'seq'), may hold values from -0.125 to 0.125
- expert_out: bfloat16 [16, 4096, 2048], P('exp', 'seq'), may hold values from -0.09375 to 0.09375
- expert_ids: int32 [16, 2048, 2], P('exp', 'seq'), may hold values from 0 to 15, all different within a row
- gate_probs: float32 [16, 2048, 2], P('exp', 'seq'), may hold values from 0.1 to 1
Outputs:
- block_out: bfloat16 [16, 2048, 2048], P('exp', 'seq')
Inputs may be any that keep to these rules, and one draw needn't show every extreme that they name: `expert_ids`: each token names 2 different experts. `window_ids`: window numbers never fall along a clip; one window of each clip holds exactly 1024 tokens and none holds more.
All inputs are finite; a program needn't handle non-finite values.
Results may differ from a plain program's by a relative error of at most 0.014.
Values may be sent and summed in bfloat16 or wider, within the bound.
No kernel may reach another device: no remote copies, remote signals or barrier semaphores. Data moves between devices by JAX's collectives and lax.ppermute only.
A program may use at most 128 MiB of HBM per device.

v0:
```python
import jax
import jax.numpy as jnp
from jax import lax
from jax.experimental import pallas as pl
from jax.experimental.pallas import tpu as pltpu
from jax.sharding import Mesh
from jax.sharding import PartitionSpec as P

HD = 64
Z = ("zh", "zl")
SEQ = ("zh", "zl", "c")
FAR = ("zh", "exp")
ROW = 8
EXTRA = 4
QB = 512
KB = 512
FLOOR = -1e30
VM = pl.BlockSpec(memory_space=pltpu.VMEM)


def step_along(array, axis, shift):
    length = lax.axis_size(axis)
    return lax.ppermute(array, axis, [(i, (i + shift) % length) for i in range(length)])


def pack_kernel(x_ref, ids_ref, o_ref):
    for i in range(o_ref.shape[0]):
        for j in range(3):
            lanes = pl.ds((16 * j + i) * 128, 128)
            o_ref[i, 128 * j : 128 * (j + 1), :] = x_ref[:, lanes]
        o_ref[i, 384:392, :] = jnp.broadcast_to(ids_ref[...].astype(jnp.float32), (8, 128)).astype(
            jnp.bfloat16
        )


def pack(head_inputs, window_ids):
    return pl.pallas_call(
        pack_kernel,
        out_shape=jax.ShapeDtypeStruct((16, 392, 128), jnp.bfloat16),
        in_specs=[VM, VM],
        out_specs=VM,
        name="pack",
    )(head_inputs, window_ids)


def attend_kernel(x_ref, o_ref, s_ref, top_ref, sum_ref, acc_ref):
    blocks, _, lanes = x_ref.shape
    tokens = blocks * 128
    ids = x_ref[:, 384:392, :][:, 0, :].astype(jnp.float32)
    edges = [jnp.sum((ids < w + 0.5).astype(jnp.float32)).astype(jnp.int32) for w in range(3)]
    first = lax.broadcasted_iota(jnp.int32, (QB, lanes), 1) < HD

    def window_of(p):
        lo, hi = edges[2], tokens
        for w in (2, 1, 0):
            inside = p < edges[w]
            lo = jnp.where(inside, edges[w - 1] if w else 0, lo)
            hi = jnp.where(inside, edges[w], hi)
        return lo, hi

    @pl.loop(0, tokens // QB)
    def _(qi):
        start = qi * QB
        q = x_ref[pl.ds(qi * (QB // 128), QB // 128), 0:128, :].reshape(QB, lanes)
        q = q * jnp.bfloat16(float(HD) ** (-0.5))
        zero = jnp.zeros_like(q)
        q2 = jnp.concatenate([jnp.where(first, q, zero), jnp.where(first, zero, q)], axis=0)
        low, _ = window_of(start)
        _, high = window_of(start + QB - 1)
        begin = low // KB
        end = (high + KB - 1) // KB
        pos = start + lax.broadcasted_iota(jnp.int32, (QB, 1), 0)
        lo, hi = window_of(jnp.concatenate([pos, pos], axis=0))
        top_ref[...] = jnp.full_like(top_ref, FLOOR)

        @pl.loop(begin, end)
        def _(kb):
            k = x_ref[pl.ds(kb * (KB // 128), KB // 128), 128:256, :].reshape(KB, lanes)
            s = lax.dot_general(
                q2, k, (((1,), (1,)), ((), ())), preferred_element_type=jnp.float32
            )
            at = kb * KB + lax.broadcasted_iota(jnp.int32, (1, KB), 1)
            s = jnp.where((at >= lo) & (at < hi), s, FLOOR)
            s_ref[kb] = s
            best = s[:, 0:128]
            for j in range(1, KB // 128):
                best = jnp.maximum(best, s[:, j * 128 : (j + 1) * 128])
            top_ref[...] = jnp.maximum(top_ref[...], best)

        top = jnp.max(top_ref[...], axis=1, keepdims=True)
        sum_ref[...] = jnp.zeros_like(sum_ref)
        acc_ref[...] = jnp.zeros_like(acc_ref)

        @pl.loop(begin, end)
        def _(kb):
            v = x_ref[pl.ds(kb * (KB // 128), KB // 128), 256:384, :].reshape(KB, lanes)
            p = jnp.exp(s_ref[kb] - top)
            part = p[:, 0:128]
            for j in range(1, KB // 128):
                part = part + p[:, j * 128 : (j + 1) * 128]
            sum_ref[...] += part
            acc_ref[...] += jnp.dot(p.astype(jnp.bfloat16), v, preferred_element_type=jnp.float32)

        out = acc_ref[...] / jnp.sum(sum_ref[...], axis=1, keepdims=True)
        out = jnp.where(first, out[:QB], out[QB:]).astype(jnp.bfloat16)
        o_ref[pl.ds(qi * (QB // 128), QB // 128)] = out.reshape(QB // 128, 128, lanes)


def attend(x):
    blocks, _, lanes = x.shape
    return pl.pallas_call(
        attend_kernel,
        out_shape=jax.ShapeDtypeStruct((blocks, 128, lanes), jnp.bfloat16),
        in_specs=[VM],
        out_specs=VM,
        scratch_shapes=[
            pltpu.VMEM((blocks * 128 // KB, 2 * QB, KB), jnp.float32),
            pltpu.VMEM((2 * QB, 128), jnp.float32),
            pltpu.VMEM((2 * QB, 128), jnp.float32),
            pltpu.VMEM((2 * QB, lanes), jnp.float32),
        ],
        compiler_params=pltpu.CompilerParams(vmem_limit_bytes=18 << 20),
        cost_estimate=pl.CostEstimate(
            flops=2 << 30, bytes_accessed=3 << 20, transcendentals=4 << 20
        ),
        name="attend",
    )(x)


def half_rows(half, width):
    row = lax.broadcasted_iota(jnp.int32, (width // 2, width), 0)
    col = lax.broadcasted_iota(jnp.int32, (width // 2, width), 1)
    same = ((col >> 3) == (row >> 2)) & ((col & 7) == (row & 3) + 4 * half)
    return same.astype(jnp.float32).astype(jnp.bfloat16)


def project_kernel(
    a_ref,
    w_ref,
    tokens_ref,
    mod_ref,
    d_ref,
    mixed_ref,
    o_ref,
    rows_ref,
    normed_ref,
    w_buf,
    sems,
):
    width = tokens_ref.shape[1]
    half = width // 2
    for n in range(width // 256):
        pltpu.make_async_copy(
            w_ref.at[:, 256 * n : 256 * (n + 1)], w_buf.at[n], sems.at[n]
        ).start()
    for i in range(a_ref.shape[0]):
        rows_ref[:, 128 * i : 128 * (i + 1)] = a_ref[i]

    @pl.loop(0, width // 256)
    def _(n):
        cols = pl.ds(pl.multiple_of(256 * n, 256), 256)
        pltpu.make_async_copy(w_buf.at[n], w_buf.at[n], sems.at[n]).wait()
        projected = jnp.dot(rows_ref[...], w_buf[n], preferred_element_type=jnp.float32)
        mixed_ref[:, cols] = (
            tokens_ref[:, cols].astype(jnp.float32) + mod_ref[0:1, cols] * projected
        )

    mixed = mixed_ref[...]
    center = jnp.mean(mixed, axis=1, keepdims=True)
    shifted = mixed - center
    spread = jnp.mean(shifted * shifted, axis=1, keepdims=True)
    normed = shifted * lax.rsqrt(spread + 1e-06)
    normed = normed * (1.0 + mod_ref[2:3, :]) + mod_ref[1:2, :]
    normed_ref[...] = normed.astype(jnp.bfloat16)
    main = d_ref.shape[0] // 2
    lower = (lax.broadcasted_iota(jnp.int32, (main, 256), 0) & EXTRA) == 0

    @pl.loop(0, half // 256)
    def _(n):
        left = pl.ds(pl.multiple_of(256 * n, 256), 256)
        right = pl.ds(pl.multiple_of(256 * n + half, 256), 256)
        last = pl.ds(pl.multiple_of(256 * n + width, 256), 256)
        first = jnp.dot(d_ref[...], normed_ref[:, left], preferred_element_type=jnp.float32)
        second = jnp.dot(d_ref[...], normed_ref[:, right], preferred_element_type=jnp.float32)
        extra = jnp.where(lower, first[main:], second[main:])
        for cols, rows in ((left, first[:main]), (right, second[:main]), (last, extra)):
            packed = rows.astype(jnp.bfloat16).reshape(main // ROW, ROW, 256)
            for copy in range(2):
                o_ref[pl.ds(copy * (main // ROW), main // ROW), :, cols] = packed


def project_and_slot(attended, out_weight, tokens, mod_rows, dispatch):
    rows, width = tokens.shape
    return pl.pallas_call(
        project_kernel,
        out_shape=(
            jax.ShapeDtypeStruct((rows, width), jnp.float32),
            jax.ShapeDtypeStruct((2 * dispatch.shape[0] // 16, ROW, 3 * width // 2), jnp.bfloat16),
        ),
        in_specs=[VM, pl.BlockSpec(memory_space=pl.ANY), VM, VM, VM],
        out_specs=(VM, VM),
        scratch_shapes=[
            pltpu.VMEM((rows, width), jnp.bfloat16),
            pltpu.VMEM((rows, width), jnp.bfloat16),
            pltpu.VMEM((width // 256, width, 256), jnp.bfloat16),
            pltpu.SemaphoreType.DMA((width // 256,)),
        ],
        compiler_params=pltpu.CompilerParams(vmem_limit_bytes=53 << 20),
        cost_estimate=pl.CostEstimate(
            flops=1 << 30, bytes_accessed=12 << 20, transcendentals=1 << 10
        ),
        name="project_and_slot",
    )(attended, out_weight, tokens, mod_rows, dispatch)


def fetch(sources, target, sems):
    return [
        pltpu.make_async_copy(source, target.at[j], sems.at[j])
        for j, source in enumerate(sources)
    ]


def activate(v):
    inner = 0.7978845608028654 * (v + 0.044715 * (v * v * v))
    return (0.5 * v * (1.0 + jnp.tanh(inner))).astype(jnp.bfloat16)


def expert_kernel(x_ref, *refs):
    count = 8
    firsts, seconds = refs[:count], refs[count : 2 * count]
    o_ref, first_buf, second_buf, rows_ref, hidden_ref, out_ref, sems = refs[2 * count :]
    blocks, _, packed = x_ref.shape
    main, width = blocks * ROW, 2048
    half = width // 2
    first_copies = fetch(firsts, first_buf, sems.at[0])
    second_copies = fetch(seconds, second_buf, sems.at[1])
    for copy in first_copies + second_copies:
        copy.start()
    rows_ref[0:main, :] = x_ref[:, :, 0:width].reshape(main, width)
    extra = x_ref[:, :, width:packed].reshape(main, half)
    for h in range(2):
        rows_ref[main:, h * half : (h + 1) * half] = jnp.dot(
            half_rows(h, main), extra, preferred_element_type=jnp.float32
        ).astype(jnp.bfloat16)

    @pl.loop(0, count)
    def _(j):
        pltpu.make_async_copy(first_buf.at[j], first_buf.at[j], sems.at[0, j]).wait()
        v = jnp.dot(rows_ref[...], first_buf[j], preferred_element_type=jnp.float32)
        hidden_ref[:, pl.ds(pl.multiple_of(256 * j, 256), 256)] = activate(v)

    for copy in second_copies:
        copy.wait()

    @pl.loop(0, width // 256)
    def _(n):
        cols = pl.ds(pl.multiple_of(256 * n, 256), 256)
        out_ref[:, cols] = jnp.dot(
            hidden_ref[...],
            second_buf[:, :, cols].reshape(256 * count, 256),
            preferred_element_type=jnp.float32,
        ).astype(jnp.bfloat16)

    o_ref[:, :, 0:width] = out_ref[0:main, :].reshape(blocks, ROW, width)
    back = None
    for h in range(2):
        part = lax.dot_general(
            half_rows(h, main),
            out_ref[main:, h * half : (h + 1) * half],
            (((0,), (0,)), ((), ())),
            preferred_element_type=jnp.float32,
        )
        back = part if back is None else back + part
    o_ref[:, :, width:packed] = back.astype(jnp.bfloat16).reshape(blocks, ROW, half)


def run_expert(arrived, firsts, seconds):
    rows, count = arrived.shape[0] * (ROW + EXTRA), len(firsts)
    anywhere = pl.BlockSpec(memory_space=pl.ANY)
    return pl.pallas_call(
        expert_kernel,
        out_shape=jax.ShapeDtypeStruct(arrived.shape, jnp.bfloat16),
        in_specs=[VM] + [anywhere] * (2 * count),
        out_specs=VM,
        scratch_shapes=[
            pltpu.VMEM((count, 2048, 256), jnp.bfloat16),
            pltpu.VMEM((count, 256, 2048), jnp.bfloat16),
            pltpu.VMEM((rows, 2048), jnp.bfloat16),
            pltpu.VMEM((rows, 256 * count), jnp.bfloat16),
            pltpu.VMEM((rows, 2048), jnp.bfloat16),
            pltpu.SemaphoreType.DMA((2, count)),
        ],
        compiler_params=pltpu.CompilerParams(vmem_limit_bytes=58 << 20),
        cost_estimate=pl.CostEstimate(
            flops=6 << 30, bytes_accessed=20 << 20, transcendentals=1 << 20
        ),
        name="run_expert",
    )(arrived, *firsts, *seconds)


def finish_kernel(r_ref, g_ref, mixed_ref, gate_ref, o_ref):
    width = mixed_ref.shape[1]
    half = width // 2
    gains = g_ref[...]
    coarse = gains.astype(jnp.bfloat16)
    fine = (gains - coarse.astype(jnp.float32)).astype(jnp.bfloat16)
    both = jnp.concatenate([coarse, fine], axis=0)
    tokens = mixed_ref.shape[0]
    lane = lax.broadcasted_iota(jnp.int32, (2 * tokens, 128), 1)
    zero = jnp.zeros((2 * tokens, 128), jnp.bfloat16)
    for h in range(2):
        total = None
        for zh in range(2):
            part = r_ref[16 * zh : 16 * (zh + 1)]
            main = part[:, :, h * half : (h + 1) * half].reshape(128, half)
            extra = part[:, :, width : width + half].reshape(128, half)
            chosen = jnp.where(((lane >> 2) & 1) == h, both[:, 128:], zero)
            more = jnp.dot(both[:, :128], main, preferred_element_type=jnp.float32)
            more = more + jnp.dot(chosen, extra, preferred_element_type=jnp.float32)
            total = more if total is None else total + more
        cols = slice(h * half, (h + 1) * half)
        combined = total[:tokens] + total[tokens:]
        o_ref[:, cols] = (mixed_ref[:, cols] + gate_ref[:, cols] * combined).astype(jnp.bfloat16)


def finish(returned, gains, mixed, gate):
    return pl.pallas_call(
        finish_kernel,
        out_shape=jax.ShapeDtypeStruct(mixed.shape, jnp.bfloat16),
        in_specs=[VM] * 4,
        out_specs=VM,
        compiler_params=pltpu.CompilerParams(vmem_limit_bytes=20 << 20),
        name="finish",
    )(returned, gains, mixed, gate)


def hop(array, turn):
    layers, cores = lax.axis_size(Z), lax.axis_size("c")
    pairs = []
    for z in range(layers):
        for c in range(cores):
            to = (z + (turn if c else -turn)) % layers
            pairs.append((z * cores + c, to * cores + c))
    return lax.ppermute(array, SEQ, pairs)


def gather_weights(first, second):
    pair = {"first": first, "second": second}
    ahead, behind, far = {}, {}, {}
    for name, w in pair.items():
        ahead[name] = hop(w, 1)
        behind[name] = hop(w, -1)
    for name, w in ahead.items():
        far[name] = hop(w, 1)
    gathered = []
    for name, w in pair.items():
        mine = [w, ahead[name], behind[name], far[name]]
        gathered.append(mine + [step_along(piece, "c", 1) for piece in mine])
    return gathered


def block(
    tokens,
    head_inputs,
    window_ids,
    modulation,
    out_weight,
    expert_in,
    expert_out,
    expert_ids,
    gate_probs,
):
    expert_count = lax.axis_size("exp")
    by_heads = lax.all_to_all(pack(head_inputs[0], window_ids), SEQ, 0, 0, tiled=True)
    firsts, seconds = gather_weights(expert_in[0], expert_out[0])
    attended = attend(by_heads)
    by_tokens = lax.all_to_all(attended, SEQ, 0, 0, tiled=True)
    mod_rows = modulation[0]
    pairs = expert_ids[0]
    pair_experts = pairs.reshape(-1)
    onehot = (pair_experts[:, None] == jnp.arange(expert_count, dtype=jnp.int32)[None, :]).astype(
        jnp.int32
    )
    before = jnp.cumsum(onehot, axis=0) - onehot
    slots = jnp.sum(before * onehot, axis=1).reshape(pairs.shape)
    place = jnp.arange(2 * expert_count * ROW, dtype=jnp.int32)
    owner = (place >> 3) & (expert_count - 1)
    slot = jnp.where(place < expert_count * ROW, place & 7, ROW + (place & 3))
    chosen = (pairs[None] == owner[:, None, None]) & (slots[None] == slot[:, None, None])
    dispatch = jnp.sum(chosen.astype(jnp.int32), axis=2).astype(jnp.bfloat16)
    picked = (pairs[:, :, None] == owner[None, None]) & (slots[:, :, None] == slot[None, None])
    gains = jnp.sum(jnp.where(picked, gate_probs[0][:, :, None], 0.0), axis=1)
    mixed_rows, outgoing = project_and_slot(by_tokens, out_weight, tokens[0], mod_rows, dispatch)
    arrived = lax.all_to_all(outgoing, FAR, 0, 0, tiled=True)
    outbound = run_expert(arrived, firsts, seconds)
    returned = lax.all_to_all(outbound, FAR, 0, 0, tiled=True)
    return finish(returned, gains, mixed_rows, mod_rows[3][None, :])[None]


def solution(mesh):
    split = Mesh(
        mesh.devices.reshape(2, 4, 2, mesh.shape["exp"]), ("zh", "zl", "c", "exp")
    )
    in_specs = (
        P("exp", SEQ, None),
        P("exp", SEQ, None),
        P("exp", SEQ),
        P("exp", None, None),
        P(),
        P("exp", None, SEQ),
        P("exp", SEQ, None),
        P("exp", SEQ, None),
        P("exp", SEQ, None),
    )
    out_specs = P("exp", SEQ, None)
    return jax.shard_map(block, mesh=split, in_specs=in_specs, out_specs=out_specs, check_vma=False)
```

profile of v0, /device:TPU:33, one launch (start us, length us, event | category | flops | bytes accessed | tf_op | source)
XLA Modules:
  0.0 262.1 jit_solution(5594395775970509155)
XLA Ops:
  0.0 2.9 %pack.1 = bf16[16,392,128]{2,1,0:T(8,128)(2,1)} custom-call(bf16[128,6144]{1,0:T(8,128)(2,1)} %bitcast.30, s32[1,128]{1,0:T(1,128)} %ids_ref.1), custom_call_target="tpu_custom_call" | custom-call | tf_op jit(solution)/shard_map/pack/pallas_call | solution.py:37
  2.9 48.8 %all_to_all.20.x_ref = bf16[16,392,128]{2,1,0:T(8,128)(2,1)S(1)} all-to-all(bf16[16,392,128]{2,1,0:T(8,128)(2,1)} %pack.1), channel_id=1, replica_groups=mesh['zh'=2,'zl'=4,'c'=2,'exp'=16] {'zh','zl','c'}, dimensions={0} | all-to-all | bytes 3211264 | tf_op jit(solution)/shard_map/all_to_all | solution.py:374
  51.6 16.0 %attend.1 = bf16[16,128,128]{2,1,0:T(8,128)(2,1)} custom-call(bf16[16,392,128]{2,1,0:T(8,128)(2,1)S(1)} %all_to_all.20.x_ref), custom_call_target="tpu_custom_call" | custom-call | flops 2147483648 | bytes 3145728 | tf_op jit(solution)/shard_map/attend/pallas_call | solution.py:111
  67.6 4.8 %all-to-all-start.1 = ((bf16[16,128,128]{2,1,0:T(8,128)(2,1)}), bf16[16,128,128]{2,1,0:T(8,128)(2,1)S(1)}, u32[]{:S(2)}, u32[]{:S(2)}) async-start(bf16[16,128,128]{2,1,0:T(8,128)(2,1)} %attend.1), calls=%async_computation.1 | async-start | bytes 1048576 | tf_op jit(solution)/shard_map/all_to_all | solution.py:377
  72.4 1.2 collective-permute-start.7
  73.9 1.2 collective-permute-start
  77.1 9.8 %all-to-all-done.1.a_ref = bf16[16,128,128]{2,1,0:T(8,128)(2,1)S(1)} async-done(((bf16[16,128,128]{2,1,0:T(8,128)(2,1)}), bf16[16,128,128]{2,1,0:T(8,128)(2,1)S(1)}, u32[]{:S(2)}, u32[]{:S(2)}) %all-to-all-start.1) | async-done | bytes 524320 | tf_op jit(solution)/shard_map/all_to_all | solution.py:377
  86.9 7.5 %project_and_slot.1 = (f32[128,2048]{1,0:T(8,128)}, bf16[32,8,3072]{2,1,0:T(8,128)(2,1)}) custom-call(bf16[16,128,128]{2,1,0:T(8,128)(2,1)S(1)} %all-to-all-done.1.a_ref, bf16[2048,2048]{1,0:T(8,128)(2,1)} %w_ref.1, bf16[128,2048]{1,0:T(8,128)(2,1)} %bitcast.31, f32[4,2048]{1,0:T(4,128)S(1)} %bitcast.29, bf16[256,128]{1,0:T(8,128)(2,1)S(1)} %convert_element_type.16.d_ref), custom_call_target="tpu_custom_call" | custom-call | flops 1073741824 | bytes 12582912 | tf_op jit(solution)/shard_map/project_and_slot/pallas_call | solution.py:194
  94.4 10.2 %all-to-all-start.2 = ((bf16[32,8,3072]{2,1,0:T(8,128)(2,1)}), bf16[32,8,3072]{2,1,0:T(8,128)(2,1)S(1)}, u32[]{:S(2)}, u32[]{:S(2)}) async-start(bf16[32,8,3072]{2,1,0:T(8,128)(2,1)} %get-tuple-element.7), calls=%async_computation.2 | async-start | bytes 3145728 | tf_op jit(solution)/shard_map/all_to_all | solution.py:394
  104.6 1.3 collective-permute-start.10
  105.9 1.6 collective-permute-done.7.refs_9_
  107.5 2.3 collective-permute-start.3
  109.8 20.1 %collective-permute-done.refs_1_ = bf16[2048,256]{1,0:T(8,128)(2,1)} collective-permute-done((bf16[2048,256]{1,0:T(8,128)(2,1)S(1)}, bf16[2048,256]{1,0:T(8,128)(2,1)}, u32[]{:S(2)}, u32[]{:S(2)}) %collective-permute-start) | collective-permute-done | bytes 1048608 | tf_op jit(solution)/shard_map/ppermute | solution.py:344
  130.0 1.6 collective-permute-start.9
  132.6 1.3 collective-permute-start.11
  134.4 40.8 %collective-permute-done.9.refs_11_ = bf16[256,2048]{1,0:T(8,128)(2,1)S(1)} collective-permute-done((bf16[256,2048]{1,0:T(8,128)(2,1)}, bf16[256,2048]{1,0:T(8,128)(2,1)S(1)}, u32[]{:S(2)}, u32[]{:S(2)}) %collective-permute-start.9) | collective-permute-done | bytes 1048608 | tf_op jit(solution)/shard_map/ppermute | solution.py:344
  175.2 2.4 collective-permute-start.5
  177.6 8.8 %collective-permute-done.2.refs_3_ = bf16[2048,256]{1,0:T(8,128)(2,1)S(1)} collective-permute-done((bf16[2048,256]{1,0:T(8,128)(2,1)}, bf16[2048,256]{1,0:T(8,128)(2,1)S(1)}, u32[]{:S(2)}, u32[]{:S(2)}) %collective-permute-start.2) | collective-permute-done | bytes 1048608 | tf_op jit(solution)/shard_map/ppermute | solution.py:344
  186.4 2.4 collective-permute-start.13
  189.0 2.1 collective-permute-done.13.refs_15_
  193.9 14.2 %run_expert.1 = bf16[32,8,3072]{2,1,0:T(8,128)(2,1)} custom-call(bf16[32,8,3072]{2,1,0:T(8,128)(2,1)} %copy-done.2, bf16[2048,256]{1,0:T(8,128)(2,1)} %bitcast.35, bf16[2048,256]{1,0:T(8,128)(2,1)} %collective-permute-done.refs_1_, bf16[2048,256]{1,0:T(8,128)(2,1)} %collective-permute-done.1.refs_2_, bf16[2048,256]{1,0:T(8,128)(2,1)} %copy-done.9, ...), custom_call_target="tpu_custom_call" | custom-call | flops 6442450944 | bytes 20971520 | tf_op jit(solution)/shard_map/run_expert/pallas_call | solution.py:280
  208.1 9.9 %all-to-all-start.3 = ((bf16[32,8,3072]{2,1,0:T(8,128)(2,1)}), bf16[32,8,3072]{2,1,0:T(8,128)(2,1)S(1)}, u32[]{:S(2)}, u32[]{:S(2)}) async-start(bf16[32,8,3072]{2,1,0:T(8,128)(2,1)} %run_expert.1), calls=%async_computation.3 | async-start | bytes 3145728 | tf_op jit(solution)/shard_map/all_to_all | solution.py:396
  218.2 41.8 %all-to-all-done.3.r_ref = bf16[32,8,3072]{2,1,0:T(8,128)(2,1)S(1)} async-done(((bf16[32,8,3072]{2,1,0:T(8,128)(2,1)}), bf16[32,8,3072]{2,1,0:T(8,128)(2,1)S(1)}, u32[]{:S(2)}, u32[]{:S(2)}) %all-to-all-start.3) | async-done | bytes 1572896 | tf_op jit(solution)/shard_map/all_to_all | solution.py:396
  260.0 2.0 finish.1
  (62 shorter events, 6.8 us)
Async XLA Ops:
  51.6 22.3 %copy-start.5 = (bf16[1,2048,256]{2,1,0:T(8,128)(2,1)S(1)}, bf16[1,2048,256]{2,1,0:T(8,128)(2,1)}, u32[]{:S(2)}) copy-start(bf16[1,2048,256]{2,1,0:T(8,128)(2,1)} %param.14) | copy-start | bytes 3145732
  51.6 23.7 %copy-start.3 = (s32[1,128,2]{1,2,0:T(2,128)S(1)}, s32[1,128,2]{1,2,0:T(2,128)}, u32[]{:S(2)}) copy-start(s32[1,128,2]{1,2,0:T(2,128)} %param.16) | copy-start | bytes 3076
  67.6 19.3 %copy-start.1 = (f32[1,4,2048]{2,1,0:T(4,128)S(1)}, f32[1,4,2048]{2,1,0:T(4,128)}, u32[]{:S(2)}) copy-start(f32[1,4,2048]{2,1,0:T(4,128)} %param.12) | copy-start | bytes 98308
  67.6 19.3 %all-to-all-start.1 = ((bf16[16,128,128]{2,1,0:T(8,128)(2,1)}), bf16[16,128,128]{2,1,0:T(8,128)(2,1)S(1)}, u32[]{:S(2)}, u32[]{:S(2)}) async-start(bf16[16,128,128]{2,1,0:T(8,128)(2,1)} %attend.1), calls=%async_computation.1 | async-start | bytes 1048576 | tf_op jit(solution)/shard_map/all_to_all | solution.py:377
  72.4 35.1 %collective-permute-start.7 = (bf16[256,2048]{1,0:T(8,128)(2,1)}, bf16[256,2048]{1,0:T(8,128)(2,1)}, u32[]{:S(2)}, u32[]{:S(2)}) collective-permute-start(bf16[256,2048]{1,0:T(8,128)(2,1)} %bitcast.6.refs_8_), channel_id=1, source_target_pairs={{0,224},{16,48},{32,0},{48,80},{64,32},{80,112},{96,64},{112,144},... | collective-permute-start | bytes 3145736 | tf_op jit(solution)/shard_map/ppermute | solution.py:344
  73.6 58.0 %collective-permute-start.8 = (bf16[256,2048]{1,0:T(8,128)(2,1)}, bf16[256,2048]{1,0:T(8,128)(2,1)}, u32[]{:S(2)}, u32[]{:S(2)}) collective-permute-start(bf16[256,2048]{1,0:T(8,128)(2,1)} %bitcast.6.refs_8_), channel_id=1, source_target_pairs={{0,32},{16,240},{32,64},{48,16},{64,96},{80,48},{96,128},{112,80},... | collective-permute-start | bytes 3145736 | tf_op jit(solution)/shard_map/ppermute | solution.py:344
  73.9 56.1 %collective-permute-start = (bf16[2048,256]{1,0:T(8,128)(2,1)S(1)}, bf16[2048,256]{1,0:T(8,128)(2,1)}, u32[]{:S(2)}, u32[]{:S(2)}) collective-permute-start(bf16[2048,256]{1,0:T(8,128)(2,1)S(1)} %bitcast.36), channel_id=1, source_target_pairs={{0,224},{16,48},{32,0},{48,80},{64,32},{80,112},{96,64},{112,144},... | collective-permute-start | bytes 3145736 | tf_op jit(solution)/shard_map/ppermute | solution.py:344
  75.1 57.5 %collective-permute-start.1 = (bf16[2048,256]{1,0:T(8,128)(2,1)S(1)}, bf16[2048,256]{1,0:T(8,128)(2,1)}, u32[]{:S(2)}, u32[]{:S(2)}) collective-permute-start(bf16[2048,256]{1,0:T(8,128)(2,1)S(1)} %bitcast.37), channel_id=1, source_target_pairs={{0,32},{16,240},{32,64},{48,16},{64,96},{80,48},{96,128},{112,80},... | collective-permute-start | bytes 3145736 | tf_op jit(solution)/shard_map/ppermute | solution.py:344
  94.4 98.3 %all-to-all-start.2 = ((bf16[32,8,3072]{2,1,0:T(8,128)(2,1)}), bf16[32,8,3072]{2,1,0:T(8,128)(2,1)S(1)}, u32[]{:S(2)}, u32[]{:S(2)}) async-start(bf16[32,8,3072]{2,1,0:T(8,128)(2,1)} %get-tuple-element.7), calls=%async_computation.2 | async-start | bytes 3145728 | tf_op jit(solution)/shard_map/all_to_all | solution.py:394
  104.6 29.3 %collective-permute-start.10 = (bf16[256,2048]{1,0:T(8,128)(2,1)}, bf16[256,2048]{1,0:T(8,128)(2,1)S(1)}, u32[]{:S(2)}, u32[]{:S(2)}) collective-permute-start(bf16[256,2048]{1,0:T(8,128)(2,1)} %bitcast.6.refs_8_), channel_id=1, source_target_pairs={{0,16},{16,0},{1,17},{17,1},{2,18},{18,2},{3,19},{19,3},{4,20},{20... | collective-permute-start | bytes 3145736 | tf_op jit(solution)/shard_map/ppermute | solution.py:23
  107.5 26.5 %collective-permute-start.3 = (bf16[2048,256]{1,0:T(8,128)(2,1)S(1)}, bf16[2048,256]{1,0:T(8,128)(2,1)S(1)}, u32[]{:S(2)}, u32[]{:S(2)}) collective-permute-start(bf16[2048,256]{1,0:T(8,128)(2,1)S(1)} %bitcast.38), channel_id=1, source_target_pairs={{0,16},{16,0},{1,17},{17,1},{2,18},{18,2},{3,19},{19,3},{4,20},{20... | collective-permute-start | bytes 3145736 | tf_op jit(solution)/shard_map/ppermute | solution.py:23
  130.0 45.2 %collective-permute-start.9 = (bf16[256,2048]{1,0:T(8,128)(2,1)}, bf16[256,2048]{1,0:T(8,128)(2,1)S(1)}, u32[]{:S(2)}, u32[]{:S(2)}) collective-permute-start(bf16[256,2048]{1,0:T(8,128)(2,1)} %collective-permute-done.7.refs_9_), channel_id=1, source_target_pairs={{0,224},{16,48},{32,0},{48,80},{64,32},{80,112},{96,64},{112,144},... | collective-permute-start | bytes 3145736 | tf_op jit(solution)/shard_map/ppermute | solution.py:344
  131.6 54.8 %collective-permute-start.2 = (bf16[2048,256]{1,0:T(8,128)(2,1)}, bf16[2048,256]{1,0:T(8,128)(2,1)S(1)}, u32[]{:S(2)}, u32[]{:S(2)}) collective-permute-start(bf16[2048,256]{1,0:T(8,128)(2,1)} %collective-permute-done.refs_1_), channel_id=1, source_target_pairs={{0,224},{16,48},{32,0},{48,80},{64,32},{80,112},{96,64},{112,144},... | collective-permute-start | bytes 3145736 | tf_op jit(solution)/shard_map/ppermute | solution.py:344
  132.6 56.3 %collective-permute-start.11 = (bf16[256,2048]{1,0:T(8,128)(2,1)}, bf16[256,2048]{1,0:T(8,128)(2,1)S(1)}, u32[]{:S(2)}, u32[]{:S(2)}) collective-permute-start(bf16[256,2048]{1,0:T(8,128)(2,1)} %collective-permute-done.7.refs_9_), channel_id=1, source_target_pairs={{0,16},{16,0},{1,17},{17,1},{2,18},{18,2},{3,19},{19,3},{4,20},{20... | collective-permute-start | bytes 3145736 | tf_op jit(solution)/shard_map/ppermute | solution.py:23
  133.9 57.2 %copy-start.6 = (bf16[256,2048]{1,0:T(8,128)(2,1)}, bf16[256,2048]{1,0:T(8,128)(2,1)S(1)}, u32[]{:S(2)}) copy-start(bf16[256,2048]{1,0:T(8,128)(2,1)S(1)} %collective-permute-done.10.refs_12_) | copy-start | bytes 3145732
  133.9 55.0 %collective-permute-start.4 = (bf16[2048,256]{1,0:T(8,128)(2,1)}, bf16[2048,256]{1,0:T(8,128)(2,1)S(1)}, u32[]{:S(2)}, u32[]{:S(2)}) collective-permute-start(bf16[2048,256]{1,0:T(8,128)(2,1)} %collective-permute-done.refs_1_), channel_id=1, source_target_pairs={{0,16},{16,0},{1,17},{17,1},{2,18},{18,2},{3,19},{19,3},{4,20},{20... | collective-permute-start | bytes 3145736 | tf_op jit(solution)/shard_map/ppermute | solution.py:23
  134.0 57.1 %copy-start.7 = (bf16[2048,256]{1,0:T(8,128)(2,1)}, bf16[2048,256]{1,0:T(8,128)(2,1)S(1)}, u32[]{:S(2)}) copy-start(bf16[2048,256]{1,0:T(8,128)(2,1)S(1)} %collective-permute-done.3.refs_4_) | copy-start | bytes 3145732
  134.0 54.9 %collective-permute-start.12 = (bf16[256,2048]{1,0:T(8,128)(2,1)}, bf16[256,2048]{1,0:T(8,128)(2,1)S(1)}, u32[]{:S(2)}, u32[]{:S(2)}) collective-permute-start(bf16[256,2048]{1,0:T(8,128)(2,1)} %collective-permute-done.8.refs_10_), channel_id=1, source_target_pairs={{0,16},{16,0},{1,17},{17,1},{2,18},{18,2},{3,19},{19,3},{4,20},{20... | collective-permute-start | bytes 3145736 | tf_op jit(solution)/shard_map/ppermute | solution.py:23
  175.2 15.9 %copy-start.8 = (bf16[256,2048]{1,0:T(8,128)(2,1)}, bf16[256,2048]{1,0:T(8,128)(2,1)S(1)}, u32[]{:S(2)}) copy-start(bf16[256,2048]{1,0:T(8,128)(2,1)S(1)} %collective-permute-done.9.refs_11_) | copy-start | bytes 3145732
  175.2 13.8 %collective-permute-start.5 = (bf16[2048,256]{1,0:T(8,128)(2,1)}, bf16[2048,256]{1,0:T(8,128)(2,1)S(1)}, u32[]{:S(2)}, u32[]{:S(2)}) collective-permute-start(bf16[2048,256]{1,0:T(8,128)(2,1)} %collective-permute-done.1.refs_2_), channel_id=1, source_target_pairs={{0,16},{16,0},{1,17},{17,1},{2,18},{18,2},{3,19},{19,3},{4,20},{20... | collective-permute-start | bytes 3145736 | tf_op jit(solution)/shard_map/ppermute | solution.py:23
  186.4 4.7 %collective-permute-start.13 = (bf16[256,2048]{1,0:T(8,128)(2,1)S(1)}, bf16[256,2048]{1,0:T(8,128)(2,1)S(1)}, u32[]{:S(2)}, u32[]{:S(2)}) collective-permute-start(bf16[256,2048]{1,0:T(8,128)(2,1)S(1)} %collective-permute-done.9.refs_11_), channel_id=1, source_target_pairs={{0,16},{16,0},{1,17},{17,1},{2,18},{18,2},{3,19},{19,3},{4,20},{20... | collective-permute-start | bytes 3145736 | tf_op jit(solution)/shard_map/ppermute | solution.py:23
  188.8 3.9 %collective-permute-start.6 = (bf16[2048,256]{1,0:T(8,128)(2,1)S(1)}, bf16[2048,256]{1,0:T(8,128)(2,1)}, u32[]{:S(2)}, u32[]{:S(2)}) collective-permute-start(bf16[2048,256]{1,0:T(8,128)(2,1)S(1)} %collective-permute-done.2.refs_3_), channel_id=1, source_target_pairs={{0,16},{16,0},{1,17},{17,1},{2,18},{18,2},{3,19},{19,3},{4,20},{20... | collective-permute-start | bytes 3145736 | tf_op jit(solution)/shard_map/ppermute | solution.py:23
  208.1 51.9 %copy-start = (f32[128,2048]{1,0:T(8,128)S(1)}, f32[128,2048]{1,0:T(8,128)}, u32[]{:S(2)}) copy-start(f32[128,2048]{1,0:T(8,128)} %get-tuple-element.8.mixed_ref) | copy-start | bytes 3145732
  208.1 51.9 %all-to-all-start.3 = ((bf16[32,8,3072]{2,1,0:T(8,128)(2,1)}), bf16[32,8,3072]{2,1,0:T(8,128)(2,1)S(1)}, u32[]{:S(2)}, u32[]{:S(2)}) async-start(bf16[32,8,3072]{2,1,0:T(8,128)(2,1)} %run_expert.1), calls=%async_computation.3 | async-start | bytes 3145728 | tf_op jit(solution)/shard_map/all_to_all | solution.py:396
  (8 other events, 27.3 us)
where the time goes:
time: 263 us; the launch traced here: 262 us
  waiting for transfers between devices  126 us (48%)
  blocking collectives  48.8 us (19%)
  Pallas kernels  42.5 us (16%)
  starting transfers between devices  40.8 us (16%)
  local copies, waits for them, and re-layouts  3 us (1%)
    ppermute x6, waiting for transfers between devices, hop(): return lax.ppermute(array, SEQ, pairs)  71.4 us
    all_to_all x1, blocking collectives, block(): lax.all_to_all(pack(head_inputs[0], window_ids), SEQ, 0, 0, tiled=True)  48.8 us
    all_to_all x1, waiting for transfers between devices, block(): returned = lax.all_to_all(outbound, FAR, 0, 0, tiled=True)  41.8 us
    pallas_call x1, Pallas kernels, attend(): pl.pallas_call(attend_kernel, out_shape=jax.ShapeDtypeStruct((blocks, 128...  16 us
    pallas_call x1, Pallas kernels, run_expert(): pl.pallas_call(expert_kernel, out_shape=jax.ShapeDtypeStruct(arrived.shap...  14.2 us
    ppermute x8, starting transfers between devices, step_along(): lax.ppermute(array, axis, [(i, (i + shift) % length) for i in range(lengt...  10.4 us
    all_to_all x1, starting transfers between devices, block(): arrived = lax.all_to_all(outgoing, FAR, 0, 0, tiled=True)  10.2 us
    all_to_all x1, starting transfers between devices, block(): returned = lax.all_to_all(outbound, FAR, 0, 0, tiled=True)  9.87 us
  transfers between devices with their start and end apart: 17, of which 8 were waited for; matrix products, arithmetic and copies ran while one was open for 1% of the time, Pallas kernels for 3%

commit v1 on v0

--- a/solution.py
+++ b/solution.py
@@ -243,23 +243,26 @@
             half_rows(h, main), extra, preferred_element_type=jnp.float32
         ).astype(jnp.bfloat16)
 
-    @pl.loop(0, count)
-    def _(j):
-        pltpu.make_async_copy(first_buf.at[j], first_buf.at[j], sems.at[0, j]).wait()
-        v = jnp.dot(rows_ref[...], first_buf[j], preferred_element_type=jnp.float32)
-        hidden_ref[:, pl.ds(pl.multiple_of(256 * j, 256), 256)] = activate(v)
+    @pl.loop(0, count // 2)
+    def _(i):
+        for j in (2 * i, 2 * i + 1):
+            pltpu.make_async_copy(first_buf.at[j], first_buf.at[j], sems.at[0, j]).wait()
+        for j in (2 * i, 2 * i + 1):
+            v = jnp.dot(rows_ref[...], first_buf[j], preferred_element_type=jnp.float32)
+            hidden_ref[:, pl.ds(pl.multiple_of(256 * j, 256), 256)] = activate(v)
 
     for copy in second_copies:
         copy.wait()
 
-    @pl.loop(0, width // 256)
-    def _(n):
-        cols = pl.ds(pl.multiple_of(256 * n, 256), 256)
-        out_ref[:, cols] = jnp.dot(
-            hidden_ref[...],
-            second_buf[:, :, cols].reshape(256 * count, 256),
-            preferred_element_type=jnp.float32,
-        ).astype(jnp.bfloat16)
+    @pl.loop(0, width // 512)
+    def _(i):
+        for n in (2 * i, 2 * i + 1):
+            cols = pl.ds(pl.multiple_of(256 * n, 256), 256)
+            out_ref[:, cols] = jnp.dot(
+                hidden_ref[...],
+                second_buf[:, :, cols].reshape(256 * count, 256),
+                preferred_element_type=jnp.float32,
+            ).astype(jnp.bfloat16)
 
     o_ref[:, :, 0:width] = out_ref[0:main, :].reshape(blocks, ROW, width)
     back = None
@@ -290,7 +293,7 @@
             pltpu.VMEM((rows, 2048), jnp.bfloat16),
             pltpu.SemaphoreType.DMA((2, count)),
         ],
-        compiler_params=pltpu.CompilerParams(vmem_limit_bytes=58 << 20),
+        compiler_params=pltpu.CompilerParams(vmem_limit_bytes=48 << 20),
         cost_estimate=pl.CostEstimate(
             flops=6 << 30, bytes_accessed=20 << 20, transcendentals=1 << 20
         ),
@@ -306,18 +309,15 @@
     fine = (gains - coarse.astype(jnp.float32)).astype(jnp.bfloat16)
     both = jnp.concatenate([coarse, fine], axis=0)
     tokens = mixed_ref.shape[0]
-    lane = lax.broadcasted_iota(jnp.int32, (2 * tokens, 128), 1)
-    zero = jnp.zeros((2 * tokens, 128), jnp.bfloat16)
+    tall = r_ref.shape[0] * ROW
+    lane = lax.broadcasted_iota(jnp.int32, (2 * tokens, tall), 1)
+    zero = jnp.zeros((2 * tokens, tall), jnp.bfloat16)
+    extra = r_ref[:, :, width : width + half].reshape(tall, half)
     for h in range(2):
-        total = None
-        for zh in range(2):
-            part = r_ref[16 * zh : 16 * (zh + 1)]
-            main = part[:, :, h * half : (h + 1) * half].reshape(128, half)
-            extra = part[:, :, width : width + half].reshape(128, half)
-            chosen = jnp.where(((lane >> 2) & 1) == h, both[:, 128:], zero)
-            more = jnp.dot(both[:, :128], main, preferred_element_type=jnp.float32)
-            more = more + jnp.dot(chosen, extra, preferred_element_type=jnp.float32)
-            total = more if total is None else total + more
+        main = r_ref[:, :, h * half : (h + 1) * half].reshape(tall, half)
+        chosen = jnp.where(((lane >> 2) & 1) == h, both[:, tall:], zero)
+        total = jnp.dot(both[:, :tall], main, preferred_element_type=jnp.float32)
+        total = total + jnp.dot(chosen, extra, preferred_element_type=jnp.float32)
         cols = slice(h * half, (h + 1) * half)
         combined = total[:tokens] + total[tokens:]
         o_ref[:, cols] = (mixed_ref[:, cols] + gate_ref[:, cols] * combined).astype(jnp.bfloat16)
@@ -388,6 +388,9 @@
     slot = jnp.where(place < expert_count * ROW, place & 7, ROW + (place & 3))
     chosen = (pairs[None] == owner[:, None, None]) & (slots[None] == slot[:, None, None])
     dispatch = jnp.sum(chosen.astype(jnp.int32), axis=2).astype(jnp.bfloat16)
+    place = jnp.arange(4 * expert_count * ROW, dtype=jnp.int32)
+    owner = (place >> 3) & (expert_count - 1)
+    slot = jnp.where(place < 2 * expert_count * ROW, place & 7, ROW + (place & 3))
     picked = (pairs[:, :, None] == owner[None, None]) & (slots[:, :, None] == slot[None, None])
     gains = jnp.sum(jnp.where(picked, gate_probs[0][:, :, None], 0.0), axis=1)
     mixed_rows, outgoing = project_and_slot(by_tokens, out_weight, tokens[0], mod_rows, dispatch)

time: 263 us -> 262 us (level)
  local copies, waits for them, and re-layouts: 3 us -> 7.03 us
  waiting for transfers between devices: 126 us -> 123 us
    unnamed x31 -> x33, local copies, waits for them, and re-layouts: 2.32 us -> 6.35 us
  transfers between devices with their start and end apart: 17 -> 17, of which waited for: 8 -> 7; matrix products, arithmetic and copies ran while one was open for 1% -> 1% of each run, Pallas kernels for 3% -> 3%
where the time goes in v1:
time: 262 us; the launch traced here: 261 us
  waiting for transfers between devices  123 us (47%)
  blocking collectives  48.8 us (19%)
  starting transfers between devices  40.7 us (16%)
  Pallas kernels  40.4 us (15%)
  local copies, waits for them, and re-layouts  7.03 us (3%)
    ppermute x6, waiting for transfers between devices, hop(): return lax.ppermute(array, SEQ, pairs)  70.4 us
    all_to_all x1, blocking collectives, block(): lax.all_to_all(pack(head_inputs[0], window_ids), SEQ, 0, 0, tiled=True)  48.8 us
    all_to_all x1, waiting for transfers between devices, block(): returned = lax.all_to_all(outbound, FAR, 0, 0, tiled=True)  41.8 us
    pallas_call x1, Pallas kernels, attend(): pl.pallas_call(attend_kernel, out_shape=jax.ShapeDtypeStruct((blocks, 128...  16 us
    pallas_call x1, Pallas kernels, run_expert(): pl.pallas_call(expert_kernel, out_shape=jax.ShapeDtypeStruct(arrived.shap...  12.5 us
    all_to_all x1, starting transfers between devices, block(): arrived = lax.all_to_all(outgoing, FAR, 0, 0, tiled=True)  10.3 us
    ppermute x8, starting transfers between devices, step_along(): lax.ppermute(array, axis, [(i, (i + shift) % length) for i in range(lengt...  10.2 us
    all_to_all x1, starting transfers between devices, block(): returned = lax.all_to_all(outbound, FAR, 0, 0, tiled=True)  9.88 us
  transfers between devices with their start and end apart: 17, of which 7 were waited for; matrix products, arithmetic and copies ran while one was open for 1% of the time, Pallas kernels for 3%

profile of v1, /device:TPU:33, one launch (start us, length us, event | category | flops | bytes accessed | tf_op | source)
XLA Modules:
  0.0 261.2 jit_solution(16225805617796138382)
XLA Ops:
  0.0 2.9 %pack.1 = bf16[16,392,128]{2,1,0:T(8,128)(2,1)} custom-call(bf16[128,6144]{1,0:T(8,128)(2,1)} %bitcast.34, s32[1,128]{1,0:T(1,128)} %ids_ref.1), custom_call_target="tpu_custom_call" | custom-call | tf_op jit(solution)/shard_map/pack/pallas_call | solution.py:37
  2.9 48.8 %all_to_all.20.x_ref = bf16[16,392,128]{2,1,0:T(8,128)(2,1)S(1)} all-to-all(bf16[16,392,128]{2,1,0:T(8,128)(2,1)} %pack.1), channel_id=1, replica_groups=mesh['zh'=2,'zl'=4,'c'=2,'exp'=16] {'zh','zl','c'}, dimensions={0} | all-to-all | bytes 3211264 | tf_op jit(solution)/shard_map/all_to_all | solution.py:374
  51.6 16.0 %attend.1 = bf16[16,128,128]{2,1,0:T(8,128)(2,1)} custom-call(bf16[16,392,128]{2,1,0:T(8,128)(2,1)S(1)} %all_to_all.20.x_ref), custom_call_target="tpu_custom_call" | custom-call | flops 2147483648 | bytes 3145728 | tf_op jit(solution)/shard_map/attend/pallas_call | solution.py:111
  67.6 4.8 %all-to-all-start.1 = ((bf16[16,128,128]{2,1,0:T(8,128)(2,1)}), bf16[16,128,128]{2,1,0:T(8,128)(2,1)S(1)}, u32[]{:S(2)}, u32[]{:S(2)}) async-start(bf16[16,128,128]{2,1,0:T(8,128)(2,1)} %attend.1), calls=%async_computation.1 | async-start | bytes 1048576 | tf_op jit(solution)/shard_map/all_to_all | solution.py:377
  72.4 1.2 collective-permute-start.7
  77.1 9.8 %all-to-all-done.1.a_ref = bf16[16,128,128]{2,1,0:T(8,128)(2,1)S(1)} async-done(((bf16[16,128,128]{2,1,0:T(8,128)(2,1)}), bf16[16,128,128]{2,1,0:T(8,128)(2,1)S(1)}, u32[]{:S(2)}, u32[]{:S(2)}) %all-to-all-start.1) | async-done | bytes 524320 | tf_op jit(solution)/shard_map/all_to_all | solution.py:377
  86.9 7.5 %project_and_slot.1 = (f32[128,2048]{1,0:T(8,128)}, bf16[32,8,3072]{2,1,0:T(8,128)(2,1)}) custom-call(bf16[16,128,128]{2,1,0:T(8,128)(2,1)S(1)} %all-to-all-done.1.a_ref, bf16[2048,2048]{1,0:T(8,128)(2,1)} %w_ref.1, bf16[128,2048]{1,0:T(8,128)(2,1)} %bitcast.35, f32[4,2048]{1,0:T(4,128)S(1)} %bitcast.29, bf16[256,128]{1,0:T(8,128)(2,1)S(1)} %convert_element_type.16.d_ref), custom_call_target="tpu_custom_call" | custom-call | flops 1073741824 | bytes 12582912 | tf_op jit(solution)/shard_map/project_and_slot/pallas_call | solution.py:194
  94.4 10.3 %all-to-all-start.2 = ((bf16[32,8,3072]{2,1,0:T(8,128)(2,1)}), bf16[32,8,3072]{2,1,0:T(8,128)(2,1)}, u32[]{:S(2)}, u32[]{:S(2)}) async-start(bf16[32,8,3072]{2,1,0:T(8,128)(2,1)} %get-tuple-element.7), calls=%async_computation.2 | async-start | bytes 3145728 | tf_op jit(solution)/shard_map/all_to_all | solution.py:397
  104.7 1.3 collective-permute-start.10
  106.0 1.5 collective-permute-done.7.refs_9_
  107.5 2.3 collective-permute-start.3
  109.8 20.1 %collective-permute-done.refs_1_ = bf16[2048,256]{1,0:T(8,128)(2,1)S(1)} collective-permute-done((bf16[2048,256]{1,0:T(8,128)(2,1)S(1)}, bf16[2048,256]{1,0:T(8,128)(2,1)S(1)}, u32[]{:S(2)}, u32[]{:S(2)}) %collective-permute-start) | collective-permute-done | bytes 1048608 | tf_op jit(solution)/shard_map/ppermute | solution.py:344
  130.0 1.6 collective-permute-start.9
  132.6 1.2 collective-permute-start.11
  135.3 39.9 %collective-permute-done.9.refs_11_ = bf16[256,2048]{1,0:T(8,128)(2,1)S(1)} collective-permute-done((bf16[256,2048]{1,0:T(8,128)(2,1)}, bf16[256,2048]{1,0:T(8,128)(2,1)S(1)}, u32[]{:S(2)}, u32[]{:S(2)}) %collective-permute-start.9) | collective-permute-done | bytes 1048608 | tf_op jit(solution)/shard_map/ppermute | solution.py:344
  175.2 2.4 collective-permute-start.5
  177.6 8.8 %collective-permute-done.2.refs_3_ = bf16[2048,256]{1,0:T(8,128)(2,1)S(1)} collective-permute-done((bf16[2048,256]{1,0:T(8,128)(2,1)S(1)}, bf16[2048,256]{1,0:T(8,128)(2,1)S(1)}, u32[]{:S(2)}, u32[]{:S(2)}) %collective-permute-start.2) | collective-permute-done | bytes 1048608 | tf_op jit(solution)/shard_map/ppermute | solution.py:344
  186.4 2.4 collective-permute-start.13
  192.8 1.2 copy-done.4
  194.0 1.2 copy-done.6
  195.2 12.5 %run_expert.1 = bf16[32,8,3072]{2,1,0:T(8,128)(2,1)} custom-call(bf16[32,8,3072]{2,1,0:T(8,128)(2,1)} %all-to-all-done.2.x_ref, bf16[2048,256]{1,0:T(8,128)(2,1)S(1)} %bitcast.33, bf16[2048,256]{1,0:T(8,128)(2,1)S(1)} %collective-permute-done.refs_1_, bf16[2048,256]{1,0:T(8,128)(2,1)} %collective-permute-done.1.refs_2_, bf16[2048,256]{1,0:T(8,128)(2,1)S(1)} %copy-done.6, ...), custom_call_target="tpu_custom_call" | custom-call | flops 6442450944 | bytes 20971520 | tf_op jit(solution)/shard_map/run_expert/pallas_call | solution.py:283
  207.8 9.9 %all-to-all-start.3 = ((bf16[32,8,3072]{2,1,0:T(8,128)(2,1)}), bf16[32,8,3072]{2,1,0:T(8,128)(2,1)S(1)}, u32[]{:S(2)}, u32[]{:S(2)}) async-start(bf16[32,8,3072]{2,1,0:T(8,128)(2,1)} %run_expert.1), calls=%async_computation.3 | async-start | bytes 3145728 | tf_op jit(solution)/shard_map/all_to_all | solution.py:399
  217.9 41.8 %all-to-all-done.3.r_ref = bf16[32,8,3072]{2,1,0:T(8,128)(2,1)S(1)} async-done(((bf16[32,8,3072]{2,1,0:T(8,128)(2,1)}), bf16[32,8,3072]{2,1,0:T(8,128)(2,1)S(1)}, u32[]{:S(2)}, u32[]{:S(2)}) %all-to-all-start.3) | async-done | bytes 1572896 | tf_op jit(solution)/shard_map/all_to_all | solution.py:399
  259.7 1.5 finish.1
  (65 shorter events, 9.9 us)
Async XLA Ops:
  51.6 22.3 %copy-start.2 = (bf16[1,2048,256]{2,1,0:T(8,128)(2,1)S(1)}, bf16[1,2048,256]{2,1,0:T(8,128)(2,1)}, u32[]{:S(2)}) copy-start(bf16[1,2048,256]{2,1,0:T(8,128)(2,1)} %param.14) | copy-start | bytes 3145732
  51.6 23.7 %copy-start.7 = (s32[1,128,2]{1,2,0:T(2,128)S(1)}, s32[1,128,2]{1,2,0:T(2,128)}, u32[]{:S(2)}) copy-start(s32[1,128,2]{1,2,0:T(2,128)} %param.16) | copy-start | bytes 3076
  67.6 19.3 %copy-start.1 = (f32[1,4,2048]{2,1,0:T(4,128)S(1)}, f32[1,4,2048]{2,1,0:T(4,128)}, u32[]{:S(2)}) copy-start(f32[1,4,2048]{2,1,0:T(4,128)} %param.12) | copy-start | bytes 98308
  67.6 19.3 %all-to-all-start.1 = ((bf16[16,128,128]{2,1,0:T(8,128)(2,1)}), bf16[16,128,128]{2,1,0:T(8,128)(2,1)S(1)}, u32[]{:S(2)}, u32[]{:S(2)}) async-start(bf16[16,128,128]{2,1,0:T(8,128)(2,1)} %attend.1), calls=%async_computation.1 | async-start | bytes 1048576 | tf_op jit(solution)/shard_map/all_to_all | solution.py:377
  72.4 35.1 %collective-permute-start.7 = (bf16[256,2048]{1,0:T(8,128)(2,1)}, bf16[256,2048]{1,0:T(8,128)(2,1)}, u32[]{:S(2)}, u32[]{:S(2)}) collective-permute-start(bf16[256,2048]{1,0:T(8,128)(2,1)} %bitcast.6.refs_8_), channel_id=1, source_target_pairs={{0,224},{16,48},{32,0},{48,80},{64,32},{80,112},{96,64},{112,144},... | collective-permute-start | bytes 3145736 | tf_op jit(solution)/shard_map/ppermute | solution.py:344
  73.6 58.0 %collective-permute-start.8 = (bf16[256,2048]{1,0:T(8,128)(2,1)}, bf16[256,2048]{1,0:T(8,128)(2,1)}, u32[]{:S(2)}, u32[]{:S(2)}) collective-permute-start(bf16[256,2048]{1,0:T(8,128)(2,1)} %bitcast.6.refs_8_), channel_id=1, source_target_pairs={{0,32},{16,240},{32,64},{48,16},{64,96},{80,48},{96,128},{112,80},... | collective-permute-start | bytes 3145736 | tf_op jit(solution)/shard_map/ppermute | solution.py:344
  73.9 56.1 %collective-permute-start = (bf16[2048,256]{1,0:T(8,128)(2,1)S(1)}, bf16[2048,256]{1,0:T(8,128)(2,1)S(1)}, u32[]{:S(2)}, u32[]{:S(2)}) collective-permute-start(bf16[2048,256]{1,0:T(8,128)(2,1)S(1)} %bitcast.30), channel_id=1, source_target_pairs={{0,224},{16,48},{32,0},{48,80},{64,32},{80,112},{96,64},{112,144},... | collective-permute-start | bytes 3145736 | tf_op jit(solution)/shard_map/ppermute | solution.py:344
  75.1 57.5 %collective-permute-start.1 = (bf16[2048,256]{1,0:T(8,128)(2,1)S(1)}, bf16[2048,256]{1,0:T(8,128)(2,1)}, u32[]{:S(2)}, u32[]{:S(2)}) collective-permute-start(bf16[2048,256]{1,0:T(8,128)(2,1)S(1)} %bitcast.31), channel_id=1, source_target_pairs={{0,32},{16,240},{32,64},{48,16},{64,96},{80,48},{96,128},{112,80},... | collective-permute-start | bytes 3145736 | tf_op jit(solution)/shard_map/ppermute | solution.py:344
  94.4 98.3 %all-to-all-start.2 = ((bf16[32,8,3072]{2,1,0:T(8,128)(2,1)}), bf16[32,8,3072]{2,1,0:T(8,128)(2,1)}, u32[]{:S(2)}, u32[]{:S(2)}) async-start(bf16[32,8,3072]{2,1,0:T(8,128)(2,1)} %get-tuple-element.7), calls=%async_computation.2 | async-start | bytes 3145728 | tf_op jit(solution)/shard_map/all_to_all | solution.py:397
  104.7 29.1 %collective-permute-start.10 = (bf16[256,2048]{1,0:T(8,128)(2,1)}, bf16[256,2048]{1,0:T(8,128)(2,1)S(1)}, u32[]{:S(2)}, u32[]{:S(2)}) collective-permute-start(bf16[256,2048]{1,0:T(8,128)(2,1)} %bitcast.6.refs_8_), channel_id=1, source_target_pairs={{0,16},{16,0},{1,17},{17,1},{2,18},{18,2},{3,19},{19,3},{4,20},{20... | collective-permute-start | bytes 3145736 | tf_op jit(solution)/shard_map/ppermute | solution.py:23
  107.5 26.4 %collective-permute-start.3 = (bf16[2048,256]{1,0:T(8,128)(2,1)S(1)}, bf16[2048,256]{1,0:T(8,128)(2,1)S(1)}, u32[]{:S(2)}, u32[]{:S(2)}) collective-permute-start(bf16[2048,256]{1,0:T(8,128)(2,1)S(1)} %bitcast.32), channel_id=1, source_target_pairs={{0,16},{16,0},{1,17},{17,1},{2,18},{18,2},{3,19},{19,3},{4,20},{20... | collective-permute-start | bytes 3145736 | tf_op jit(solution)/shard_map/ppermute | solution.py:23
  130.0 45.2 %collective-permute-start.9 = (bf16[256,2048]{1,0:T(8,128)(2,1)}, bf16[256,2048]{1,0:T(8,128)(2,1)S(1)}, u32[]{:S(2)}, u32[]{:S(2)}) collective-permute-start(bf16[256,2048]{1,0:T(8,128)(2,1)} %collective-permute-done.7.refs_9_), channel_id=1, source_target_pairs={{0,224},{16,48},{32,0},{48,80},{64,32},{80,112},{96,64},{112,144},... | collective-permute-start | bytes 3145736 | tf_op jit(solution)/shard_map/ppermute | solution.py:344
  131.6 54.8 %collective-permute-start.2 = (bf16[2048,256]{1,0:T(8,128)(2,1)S(1)}, bf16[2048,256]{1,0:T(8,128)(2,1)S(1)}, u32[]{:S(2)}, u32[]{:S(2)}) collective-permute-start(bf16[2048,256]{1,0:T(8,128)(2,1)S(1)} %collective-permute-done.refs_1_), channel_id=1, source_target_pairs={{0,224},{16,48},{32,0},{48,80},{64,32},{80,112},{96,64},{112,144},... | collective-permute-start | bytes 3145736 | tf_op jit(solution)/shard_map/ppermute | solution.py:344
  132.6 56.3 %collective-permute-start.11 = (bf16[256,2048]{1,0:T(8,128)(2,1)}, bf16[256,2048]{1,0:T(8,128)(2,1)S(1)}, u32[]{:S(2)}, u32[]{:S(2)}) collective-permute-start(bf16[256,2048]{1,0:T(8,128)(2,1)} %collective-permute-done.7.refs_9_), channel_id=1, source_target_pairs={{0,16},{16,0},{1,17},{17,1},{2,18},{18,2},{3,19},{19,3},{4,20},{20... | collective-permute-start | bytes 3145736 | tf_op jit(solution)/shard_map/ppermute | solution.py:23
  133.8 56.2 %copy-start.9 = (bf16[256,2048]{1,0:T(8,128)(2,1)}, bf16[256,2048]{1,0:T(8,128)(2,1)S(1)}, u32[]{:S(2)}) copy-start(bf16[256,2048]{1,0:T(8,128)(2,1)S(1)} %collective-permute-done.10.refs_12_) | copy-start | bytes 3145732
  133.8 56.2 %collective-permute-start.4 = (bf16[2048,256]{1,0:T(8,128)(2,1)S(1)}, bf16[2048,256]{1,0:T(8,128)(2,1)S(1)}, u32[]{:S(2)}, u32[]{:S(2)}) collective-permute-start(bf16[2048,256]{1,0:T(8,128)(2,1)S(1)} %collective-permute-done.refs_1_), channel_id=1, source_target_pairs={{0,16},{16,0},{1,17},{17,1},{2,18},{18,2},{3,19},{19,3},{4,20},{20... | collective-permute-start | bytes 3145736 | tf_op jit(solution)/shard_map/ppermute | solution.py:23
  135.0 55.1 %collective-permute-start.12 = (bf16[256,2048]{1,0:T(8,128)(2,1)}, bf16[256,2048]{1,0:T(8,128)(2,1)S(1)}, u32[]{:S(2)}, u32[]{:S(2)}) collective-permute-start(bf16[256,2048]{1,0:T(8,128)(2,1)} %collective-permute-done.8.refs_10_), channel_id=1, source_target_pairs={{0,16},{16,0},{1,17},{17,1},{2,18},{18,2},{3,19},{19,3},{4,20},{20... | collective-permute-start | bytes 3145736 | tf_op jit(solution)/shard_map/ppermute | solution.py:23
  175.2 14.8 %copy-start.10 = (bf16[256,2048]{1,0:T(8,128)(2,1)}, bf16[256,2048]{1,0:T(8,128)(2,1)S(1)}, u32[]{:S(2)}) copy-start(bf16[256,2048]{1,0:T(8,128)(2,1)S(1)} %collective-permute-done.9.refs_11_) | copy-start | bytes 3145732
  175.2 14.8 %collective-permute-start.5 = (bf16[2048,256]{1,0:T(8,128)(2,1)}, bf16[2048,256]{1,0:T(8,128)(2,1)S(1)}, u32[]{:S(2)}, u32[]{:S(2)}) collective-permute-start(bf16[2048,256]{1,0:T(8,128)(2,1)} %collective-permute-done.1.refs_2_), channel_id=1, source_target_pairs={{0,16},{16,0},{1,17},{17,1},{2,18},{18,2},{3,19},{19,3},{4,20},{20... | collective-permute-start | bytes 3145736 | tf_op jit(solution)/shard_map/ppermute | solution.py:23
  186.4 4.7 %collective-permute-start.13 = (bf16[256,2048]{1,0:T(8,128)(2,1)S(1)}, bf16[256,2048]{1,0:T(8,128)(2,1)S(1)}, u32[]{:S(2)}, u32[]{:S(2)}) collective-permute-start(bf16[256,2048]{1,0:T(8,128)(2,1)S(1)} %collective-permute-done.9.refs_11_), channel_id=1, source_target_pairs={{0,16},{16,0},{1,17},{17,1},{2,18},{18,2},{3,19},{19,3},{4,20},{20... | collective-permute-start | bytes 3145736 | tf_op jit(solution)/shard_map/ppermute | solution.py:23
  188.8 3.9 %collective-permute-start.6 = (bf16[2048,256]{1,0:T(8,128)(2,1)S(1)}, bf16[2048,256]{1,0:T(8,128)(2,1)}, u32[]{:S(2)}, u32[]{:S(2)}) collective-permute-start(bf16[2048,256]{1,0:T(8,128)(2,1)S(1)} %collective-permute-done.2.refs_3_), channel_id=1, source_target_pairs={{0,16},{16,0},{1,17},{17,1},{2,18},{18,2},{3,19},{19,3},{4,20},{20... | collective-permute-start | bytes 3145736 | tf_op jit(solution)/shard_map/ppermute | solution.py:23
  207.8 9.9 %copy-start.8 = (f32[1,128,2]{1,2,0:T(2,128)S(1)}, f32[1,128,2]{1,2,0:T(2,128)}, u32[]{:S(2)}) copy-start(f32[1,128,2]{1,2,0:T(2,128)} %param.17) | copy-start | bytes 3076
  207.8 51.9 %copy-start = (f32[128,2048]{1,0:T(8,128)S(1)}, f32[128,2048]{1,0:T(8,128)}, u32[]{:S(2)}) copy-start(f32[128,2048]{1,0:T(8,128)} %get-tuple-element.8.mixed_ref) | copy-start | bytes 3145732
  207.8 51.9 %all-to-all-start.3 = ((bf16[32,8,3072]{2,1,0:T(8,128)(2,1)}), bf16[32,8,3072]{2,1,0:T(8,128)(2,1)S(1)}, u32[]{:S(2)}, u32[]{:S(2)}) async-start(bf16[32,8,3072]{2,1,0:T(8,128)(2,1)} %run_expert.1), calls=%async_computation.3 | async-start | bytes 3145728 | tf_op jit(solution)/shard_map/all_to_all | solution.py:399
  (9 other events, 12.0 us)

commit v2 on v1

--- a/solution.py
+++ b/solution.py
@@ -243,20 +243,20 @@
             half_rows(h, main), extra, preferred_element_type=jnp.float32
         ).astype(jnp.bfloat16)
 
-    @pl.loop(0, count // 2)
+    @pl.loop(0, count // 4)
     def _(i):
-        for j in (2 * i, 2 * i + 1):
+        for j in (4 * i, 4 * i + 1, 4 * i + 2, 4 * i + 3):
             pltpu.make_async_copy(first_buf.at[j], first_buf.at[j], sems.at[0, j]).wait()
-        for j in (2 * i, 2 * i + 1):
+        for j in (4 * i, 4 * i + 1, 4 * i + 2, 4 * i + 3):
             v = jnp.dot(rows_ref[...], first_buf[j], preferred_element_type=jnp.float32)
             hidden_ref[:, pl.ds(pl.multiple_of(256 * j, 256), 256)] = activate(v)
 
     for copy in second_copies:
         copy.wait()
 
-    @pl.loop(0, width // 512)
+    @pl.loop(0, width // 1024)
     def _(i):
-        for n in (2 * i, 2 * i + 1):
+        for n in (4 * i, 4 * i + 1, 4 * i + 2, 4 * i + 3):
             cols = pl.ds(pl.multiple_of(256 * n, 256), 256)
             out_ref[:, cols] = jnp.dot(
                 hidden_ref[...],

time: 262 us -> 262 us (level)
  no operation moved by 1% of the time
where the time goes in v2:
time: 262 us; the launch traced here: 261 us
  waiting for transfers between devices  123 us (47%)
  blocking collectives  48.8 us (19%)
  starting transfers between devices  40.7 us (16%)
  Pallas kernels  40.4 us (15%)
  local copies, waits for them, and re-layouts  7.03 us (3%)
    ppermute x6, waiting for transfers between devices, hop(): return lax.ppermute(array, SEQ, pairs)  70.4 us
    all_to_all x1, blocking collectives, block(): lax.all_to_all(pack(head_inputs[0], window_ids), SEQ, 0, 0, tiled=True)  48.8 us
    all_to_all x1, waiting for transfers between devices, block(): returned = lax.all_to_all(outbound, FAR, 0, 0, tiled=True)  41.8 us
    pallas_call x1, Pallas kernels, attend(): pl.pallas_call(attend_kernel, out_shape=jax.ShapeDtypeStruct((blocks, 128...  16 us
    pallas_call x1, Pallas kernels, run_expert(): pl.pallas_call(expert_kernel, out_shape=jax.ShapeDtypeStruct(arrived.shap...  12.6 us
    all_to_all x1, starting transfers between devices, block(): arrived = lax.all_to_all(outgoing, FAR, 0, 0, tiled=True)  10.3 us
    ppermute x8, starting transfers between devices, step_along(): lax.ppermute(array, axis, [(i, (i + shift) % length) for i in range(lengt...  10.2 us
    all_to_all x1, starting transfers between devices, block(): returned = lax.all_to_all(outbound, FAR, 0, 0, tiled=True)  9.88 us
  transfers between devices with their start and end apart: 17, of which 7 were waited for; matrix products, arithmetic and copies ran while one was open for 1% of the time, Pallas kernels for 3%

profile of v2, /device:TPU:33, one launch (start us, length us, event | category | flops | bytes accessed | tf_op | source)
XLA Modules:
  0.0 261.2 jit_solution(980163245502067405)
XLA Ops:
  0.0 2.9 %pack.1 = bf16[16,392,128]{2,1,0:T(8,128)(2,1)} custom-call(bf16[128,6144]{1,0:T(8,128)(2,1)} %bitcast.34, s32[1,128]{1,0:T(1,128)} %ids_ref.1), custom_call_target="tpu_custom_call" | custom-call | tf_op jit(solution)/shard_map/pack/pallas_call | solution.py:37
  2.9 48.8 %all_to_all.20.x_ref = bf16[16,392,128]{2,1,0:T(8,128)(2,1)S(1)} all-to-all(bf16[16,392,128]{2,1,0:T(8,128)(2,1)} %pack.1), channel_id=1, replica_groups=mesh['zh'=2,'zl'=4,'c'=2,'exp'=16] {'zh','zl','c'}, dimensions={0} | all-to-all | bytes 3211264 | tf_op jit(solution)/shard_map/all_to_all | solution.py:374
  51.6 16.0 %attend.1 = bf16[16,128,128]{2,1,0:T(8,128)(2,1)} custom-call(bf16[16,392,128]{2,1,0:T(8,128)(2,1)S(1)} %all_to_all.20.x_ref), custom_call_target="tpu_custom_call" | custom-call | flops 2147483648 | bytes 3145728 | tf_op jit(solution)/shard_map/attend/pallas_call | solution.py:111
  67.6 4.8 %all-to-all-start.1 = ((bf16[16,128,128]{2,1,0:T(8,128)(2,1)}), bf16[16,128,128]{2,1,0:T(8,128)(2,1)S(1)}, u32[]{:S(2)}, u32[]{:S(2)}) async-start(bf16[16,128,128]{2,1,0:T(8,128)(2,1)} %attend.1), calls=%async_computation.1 | async-start | bytes 1048576 | tf_op jit(solution)/shard_map/all_to_all | solution.py:377
  72.4 1.2 collective-permute-start.7
  77.1 9.8 %all-to-all-done.1.a_ref = bf16[16,128,128]{2,1,0:T(8,128)(2,1)S(1)} async-done(((bf16[16,128,128]{2,1,0:T(8,128)(2,1)}), bf16[16,128,128]{2,1,0:T(8,128)(2,1)S(1)}, u32[]{:S(2)}, u32[]{:S(2)}) %all-to-all-start.1) | async-done | bytes 524320 | tf_op jit(solution)/shard_map/all_to_all | solution.py:377
  86.9 7.5 %project_and_slot.1 = (f32[128,2048]{1,0:T(8,128)}, bf16[32,8,3072]{2,1,0:T(8,128)(2,1)}) custom-call(bf16[16,128,128]{2,1,0:T(8,128)(2,1)S(1)} %all-to-all-done.1.a_ref, bf16[2048,2048]{1,0:T(8,128)(2,1)} %w_ref.1, bf16[128,2048]{1,0:T(8,128)(2,1)} %bitcast.35, f32[4,2048]{1,0:T(4,128)S(1)} %bitcast.29, bf16[256,128]{1,0:T(8,128)(2,1)S(1)} %convert_element_type.16.d_ref), custom_call_target="tpu_custom_call" | custom-call | flops 1073741824 | bytes 12582912 | tf_op jit(solution)/shard_map/project_and_slot/pallas_call | solution.py:194
  94.4 10.3 %all-to-all-start.2 = ((bf16[32,8,3072]{2,1,0:T(8,128)(2,1)}), bf16[32,8,3072]{2,1,0:T(8,128)(2,1)}, u32[]{:S(2)}, u32[]{:S(2)}) async-start(bf16[32,8,3072]{2,1,0:T(8,128)(2,1)} %get-tuple-element.7), calls=%async_computation.2 | async-start | bytes 3145728 | tf_op jit(solution)/shard_map/all_to_all | solution.py:397
  104.7 1.3 collective-permute-start.10
  106.0 1.5 collective-permute-done.7.refs_9_
  107.5 2.3 collective-permute-start.3
  109.8 20.1 %collective-permute-done.refs_1_ = bf16[2048,256]{1,0:T(8,128)(2,1)S(1)} collective-permute-done((bf16[2048,256]{1,0:T(8,128)(2,1)S(1)}, bf16[2048,256]{1,0:T(8,128)(2,1)S(1)}, u32[]{:S(2)}, u32[]{:S(2)}) %collective-permute-start) | collective-permute-done | bytes 1048608 | tf_op jit(solution)/shard_map/ppermute | solution.py:344
  130.0 1.6 collective-permute-start.9
  132.6 1.2 collective-permute-start.11
  135.3 39.9 %collective-permute-done.9.refs_11_ = bf16[256,2048]{1,0:T(8,128)(2,1)S(1)} collective-permute-done((bf16[256,2048]{1,0:T(8,128)(2,1)}, bf16[256,2048]{1,0:T(8,128)(2,1)S(1)}, u32[]{:S(2)}, u32[]{:S(2)}) %collective-permute-start.9) | collective-permute-done | bytes 1048608 | tf_op jit(solution)/shard_map/ppermute | solution.py:344
  175.2 2.4 collective-permute-start.5
  177.6 8.8 %collective-permute-done.2.refs_3_ = bf16[2048,256]{1,0:T(8,128)(2,1)S(1)} collective-permute-done((bf16[2048,256]{1,0:T(8,128)(2,1)S(1)}, bf16[2048,256]{1,0:T(8,128)(2,1)S(1)}, u32[]{:S(2)}, u32[]{:S(2)}) %collective-permute-start.2) | collective-permute-done | bytes 1048608 | tf_op jit(solution)/shard_map/ppermute | solution.py:344
  186.4 2.4 collective-permute-start.13
  192.8 1.2 copy-done.4
  194.0 1.2 copy-done.6
  195.2 12.6 %run_expert.1 = bf16[32,8,3072]{2,1,0:T(8,128)(2,1)} custom-call(bf16[32,8,3072]{2,1,0:T(8,128)(2,1)} %all-to-all-done.2.x_ref, bf16[2048,256]{1,0:T(8,128)(2,1)S(1)} %bitcast.33, bf16[2048,256]{1,0:T(8,128)(2,1)S(1)} %collective-permute-done.refs_1_, bf16[2048,256]{1,0:T(8,128)(2,1)} %collective-permute-done.1.refs_2_, bf16[2048,256]{1,0:T(8,128)(2,1)S(1)} %copy-done.6, ...), custom_call_target="tpu_custom_call" | custom-call | flops 6442450944 | bytes 20971520 | tf_op jit(solution)/shard_map/run_expert/pallas_call | solution.py:283
  207.9 9.9 %all-to-all-start.3 = ((bf16[32,8,3072]{2,1,0:T(8,128)(2,1)}), bf16[32,8,3072]{2,1,0:T(8,128)(2,1)S(1)}, u32[]{:S(2)}, u32[]{:S(2)}) async-start(bf16[32,8,3072]{2,1,0:T(8,128)(2,1)} %run_expert.1), calls=%async_computation.3 | async-start | bytes 3145728 | tf_op jit(solution)/shard_map/all_to_all | solution.py:399
  218.0 41.8 %all-to-all-done.3.r_ref = bf16[32,8,3072]{2,1,0:T(8,128)(2,1)S(1)} async-done(((bf16[32,8,3072]{2,1,0:T(8,128)(2,1)}), bf16[32,8,3072]{2,1,0:T(8,128)(2,1)S(1)}, u32[]{:S(2)}, u32[]{:S(2)}) %all-to-all-start.3) | async-done | bytes 1572896 | tf_op jit(solution)/shard_map/all_to_all | solution.py:399
  259.7 1.5 finish.1
  (65 shorter events, 9.9 us)
Async XLA Ops:
  51.6 22.3 %copy-start.2 = (bf16[1,2048,256]{2,1,0:T(8,128)(2,1)S(1)}, bf16[1,2048,256]{2,1,0:T(8,128)(2,1)}, u32[]{:S(2)}) copy-start(bf16[1,2048,256]{2,1,0:T(8,128)(2,1)} %param.14) | copy-start | bytes 3145732
  51.6 23.7 %copy-start.7 = (s32[1,128,2]{1,2,0:T(2,128)S(1)}, s32[1,128,2]{1,2,0:T(2,128)}, u32[]{:S(2)}) copy-start(s32[1,128,2]{1,2,0:T(2,128)} %param.16) | copy-start | bytes 3076
  67.6 19.3 %copy-start.1 = (f32[1,4,2048]{2,1,0:T(4,128)S(1)}, f32[1,4,2048]{2,1,0:T(4,128)}, u32[]{:S(2)}) copy-start(f32[1,4,2048]{2,1,0:T(4,128)} %param.12) | copy-start | bytes 98308
  67.6 19.3 %all-to-all-start.1 = ((bf16[16,128,128]{2,1,0:T(8,128)(2,1)}), bf16[16,128,128]{2,1,0:T(8,128)(2,1)S(1)}, u32[]{:S(2)}, u32[]{:S(2)}) async-start(bf16[16,128,128]{2,1,0:T(8,128)(2,1)} %attend.1), calls=%async_computation.1 | async-start | bytes 1048576 | tf_op jit(solution)/shard_map/all_to_all | solution.py:377
  72.4 35.1 %collective-permute-start.7 = (bf16[256,2048]{1,0:T(8,128)(2,1)}, bf16[256,2048]{1,0:T(8,128)(2,1)}, u32[]{:S(2)}, u32[]{:S(2)}) collective-permute-start(bf16[256,2048]{1,0:T(8,128)(2,1)} %bitcast.6.refs_8_), channel_id=1, source_target_pairs={{0,224},{16,48},{32,0},{48,80},{64,32},{80,112},{96,64},{112,144},... | collective-permute-start | bytes 3145736 | tf_op jit(solution)/shard_map/ppermute | solution.py:344
  73.6 58.0 %collective-permute-start.8 = (bf16[256,2048]{1,0:T(8,128)(2,1)}, bf16[256,2048]{1,0:T(8,128)(2,1)}, u32[]{:S(2)}, u32[]{:S(2)}) collective-permute-start(bf16[256,2048]{1,0:T(8,128)(2,1)} %bitcast.6.refs_8_), channel_id=1, source_target_pairs={{0,32},{16,240},{32,64},{48,16},{64,96},{80,48},{96,128},{112,80},... | collective-permute-start | bytes 3145736 | tf_op jit(solution)/shard_map/ppermute | solution.py:344
  73.9 56.1 %collective-permute-start = (bf16[2048,256]{1,0:T(8,128)(2,1)S(1)}, bf16[2048,256]{1,0:T(8,128)(2,1)S(1)}, u32[]{:S(2)}, u32[]{:S(2)}) collective-permute-start(bf16[2048,256]{1,0:T(8,128)(2,1)S(1)} %bitcast.30), channel_id=1, source_target_pairs={{0,224},{16,48},{32,0},{48,80},{64,32},{80,112},{96,64},{112,144},... | collective-permute-start | bytes 3145736 | tf_op jit(solution)/shard_map/ppermute | solution.py:344
  75.1 57.5 %collective-permute-start.1 = (bf16[2048,256]{1,0:T(8,128)(2,1)S(1)}, bf16[2048,256]{1,0:T(8,128)(2,1)}, u32[]{:S(2)}, u32[]{:S(2)}) collective-permute-start(bf16[2048,256]{1,0:T(8,128)(2,1)S(1)} %bitcast.31), channel_id=1, source_target_pairs={{0,32},{16,240},{32,64},{48,16},{64,96},{80,48},{96,128},{112,80},... | collective-permute-start | bytes 3145736 | tf_op jit(solution)/shard_map/ppermute | solution.py:344
  94.4 98.3 %all-to-all-start.2 = ((bf16[32,8,3072]{2,1,0:T(8,128)(2,1)}), bf16[32,8,3072]{2,1,0:T(8,128)(2,1)}, u32[]{:S(2)}, u32[]{:S(2)}) async-start(bf16[32,8,3072]{2,1,0:T(8,128)(2,1)} %get-tuple-element.7), calls=%async_computation.2 | async-start | bytes 3145728 | tf_op jit(solution)/shard_map/all_to_all | solution.py:397
  104.7 29.1 %collective-permute-start.10 = (bf16[256,2048]{1,0:T(8,128)(2,1)}, bf16[256,2048]{1,0:T(8,128)(2,1)S(1)}, u32[]{:S(2)}, u32[]{:S(2)}) collective-permute-start(bf16[256,2048]{1,0:T(8,128)(2,1)} %bitcast.6.refs_8_), channel_id=1, source_target_pairs={{0,16},{16,0},{1,17},{17,1},{2,18},{18,2},{3,19},{19,3},{4,20},{20... | collective-permute-start | bytes 3145736 | tf_op jit(solution)/shard_map/ppermute | solution.py:23
  107.5 26.4 %collective-permute-start.3 = (bf16[2048,256]{1,0:T(8,128)(2,1)S(1)}, bf16[2048,256]{1,0:T(8,128)(2,1)S(1)}, u32[]{:S(2)}, u32[]{:S(2)}) collective-permute-start(bf16[2048,256]{1,0:T(8,128)(2,1)S(1)} %bitcast.32), channel_id=1, source_target_pairs={{0,16},{16,0},{1,17},{17,1},{2,18},{18,2},{3,19},{19,3},{4,20},{20... | collective-permute-start | bytes 3145736 | tf_op jit(solution)/shard_map/ppermute | solution.py:23
  130.0 45.2 %collective-permute-start.9 = (bf16[256,2048]{1,0:T(8,128)(2,1)}, bf16[256,2048]{1,0:T(8,128)(2,1)S(1)}, u32[]{:S(2)}, u32[]{:S(2)}) collective-permute-start(bf16[256,2048]{1,0:T(8,128)(2,1)} %collective-permute-done.7.refs_9_), channel_id=1, source_target_pairs={{0,224},{16,48},{32,0},{48,80},{64,32},{80,112},{96,64},{112,144},... | collective-permute-start | bytes 3145736 | tf_op jit(solution)/shard_map/ppermute | solution.py:344
  131.6 54.8 %collective-permute-start.2 = (bf16[2048,256]{1,0:T(8,128)(2,1)S(1)}, bf16[2048,256]{1,0:T(8,128)(2,1)S(1)}, u32[]{:S(2)}, u32[]{:S(2)}) collective-permute-start(bf16[2048,256]{1,0:T(8,128)(2,1)S(1)} %collective-permute-done.refs_1_), channel_id=1, source_target_pairs={{0,224},{16,48},{32,0},{48,80},{64,32},{80,112},{96,64},{112,144},... | collective-permute-start | bytes 3145736 | tf_op jit(solution)/shard_map/ppermute | solution.py:344
  132.6 56.3 %collective-permute-start.11 = (bf16[256,2048]{1,0:T(8,128)(2,1)}, bf16[256,2048]{1,0:T(8,128)(2,1)S(1)}, u32[]{:S(2)}, u32[]{:S(2)}) collective-permute-start(bf16[256,2048]{1,0:T(8,128)(2,1)} %collective-permute-done.7.refs_9_), channel_id=1, source_target_pairs={{0,16},{16,0},{1,17},{17,1},{2,18},{18,2},{3,19},{19,3},{4,20},{20... | collective-permute-start | bytes 3145736 | tf_op jit(solution)/shard_map/ppermute | solution.py:23
  133.8 56.2 %copy-start.9 = (bf16[256,2048]{1,0:T(8,128)(2,1)}, bf16[256,2048]{1,0:T(8,128)(2,1)S(1)}, u32[]{:S(2)}) copy-start(bf16[256,2048]{1,0:T(8,128)(2,1)S(1)} %collective-permute-done.10.refs_12_) | copy-start | bytes 3145732
  133.8 56.2 %collective-permute-start.4 = (bf16[2048,256]{1,0:T(8,128)(2,1)S(1)}, bf16[2048,256]{1,0:T(8,128)(2,1)S(1)}, u32[]{:S(2)}, u32[]{:S(2)}) collective-permute-start(bf16[2048,256]{1,0:T(8,128)(2,1)S(1)} %collective-permute-done.refs_1_), channel_id=1, source_target_pairs={{0,16},{16,0},{1,17},{17,1},{2,18},{18,2},{3,19},{19,3},{4,20},{20... | collective-permute-start | bytes 3145736 | tf_op jit(solution)/shard_map/ppermute | solution.py:23
  135.0 55.1 %collective-permute-start.12 = (bf16[256,2048]{1,0:T(8,128)(2,1)}, bf16[256,2048]{1,0:T(8,128)(2,1)S(1)}, u32[]{:S(2)}, u32[]{:S(2)}) collective-permute-start(bf16[256,2048]{1,0:T(8,128)(2,1)} %collective-permute-done.8.refs_10_), channel_id=1, source_target_pairs={{0,16},{16,0},{1,17},{17,1},{2,18},{18,2},{3,19},{19,3},{4,20},{20... | collective-permute-start | bytes 3145736 | tf_op jit(solution)/shard_map/ppermute | solution.py:23
  175.2 14.8 %copy-start.10 = (bf16[256,2048]{1,0:T(8,128)(2,1)}, bf16[256,2048]{1,0:T(8,128)(2,1)S(1)}, u32[]{:S(2)}) copy-start(bf16[256,2048]{1,0:T(8,128)(2,1)S(1)} %collective-permute-done.9.refs_11_) | copy-start | bytes 3145732
  175.2 14.8 %collective-permute-start.5 = (bf16[2048,256]{1,0:T(8,128)(2,1)}, bf16[2048,256]{1,0:T(8,128)(2,1)S(1)}, u32[]{:S(2)}, u32[]{:S(2)}) collective-permute-start(bf16[2048,256]{1,0:T(8,128)(2,1)} %collective-permute-done.1.refs_2_), channel_id=1, source_target_pairs={{0,16},{16,0},{1,17},{17,1},{2,18},{18,2},{3,19},{19,3},{4,20},{20... | collective-permute-start | bytes 3145736 | tf_op jit(solution)/shard_map/ppermute | solution.py:23
  186.4 4.7 %collective-permute-start.13 = (bf16[256,2048]{1,0:T(8,128)(2,1)S(1)}, bf16[256,2048]{1,0:T(8,128)(2,1)S(1)}, u32[]{:S(2)}, u32[]{:S(2)}) collective-permute-start(bf16[256,2048]{1,0:T(8,128)(2,1)S(1)} %collective-permute-done.9.refs_11_), channel_id=1, source_target_pairs={{0,16},{16,0},{1,17},{17,1},{2,18},{18,2},{3,19},{19,3},{4,20},{20... | collective-permute-start | bytes 3145736 | tf_op jit(solution)/shard_map/ppermute | solution.py:23
  188.8 3.9 %collective-permute-start.6 = (bf16[2048,256]{1,0:T(8,128)(2,1)S(1)}, bf16[2048,256]{1,0:T(8,128)(2,1)}, u32[]{:S(2)}, u32[]{:S(2)}) collective-permute-start(bf16[2048,256]{1,0:T(8,128)(2,1)S(1)} %collective-permute-done.2.refs_3_), channel_id=1, source_target_pairs={{0,16},{16,0},{1,17},{17,1},{2,18},{18,2},{3,19},{19,3},{4,20},{20... | collective-permute-start | bytes 3145736 | tf_op jit(solution)/shard_map/ppermute | solution.py:23
  207.8 9.9 %copy-start.8 = (f32[1,128,2]{1,2,0:T(2,128)S(1)}, f32[1,128,2]{1,2,0:T(2,128)}, u32[]{:S(2)}) copy-start(f32[1,128,2]{1,2,0:T(2,128)} %param.17) | copy-start | bytes 3076
  207.8 51.9 %copy-start = (f32[128,2048]{1,0:T(8,128)S(1)}, f32[128,2048]{1,0:T(8,128)}, u32[]{:S(2)}) copy-start(f32[128,2048]{1,0:T(8,128)} %get-tuple-element.8.mixed_ref) | copy-start | bytes 3145732
  207.9 51.9 %all-to-all-start.3 = ((bf16[32,8,3072]{2,1,0:T(8,128)(2,1)}), bf16[32,8,3072]{2,1,0:T(8,128)(2,1)S(1)}, u32[]{:S(2)}, u32[]{:S(2)}) async-start(bf16[32,8,3072]{2,1,0:T(8,128)(2,1)} %run_expert.1), calls=%async_computation.3 | async-start | bytes 3145728 | tf_op jit(solution)/shard_map/all_to_all | solution.py:399
  (9 other events, 12.0 us)
